TPU v7x, 256 devices: a whole 4x4x8 slice. The times are simulated.
256 devices in a mesh: seq: 64 (over x_lo, y, z), sub: 4 (over x_hi, core).
Axes of the slice: x: 4 (x_hi: 2, x_lo: 2; x = x_hi * 2 + x_lo), y: 4, z: 8, core: 2. Of those that a mesh axis runs over, the one named last changes fastest.
Arguments:
- normed: bfloat16 [32768, 2048], P(('seq', 'sub')), as said below
- w_query: bfloat16 [2048, 2048], P(None, 'sub'), as said below
- w_key: bfloat16 [2048, 2048], P(None, 'sub'), as said below
- w_value: bfloat16 [2048, 2048], P(None, 'sub'), may hold values from -0.125 to 0.125
- w_out: bfloat16 [2048, 2048], P('sub'), may hold values from -0.25 to 0.25
- pattern: int32 [16, 128], P('sub'), may hold values from 0 to 127, each once within a row
- slide_lengths: int32 [8], replicated, may hold values from 1 to 160, 256 in all
Outputs:
- mixed: bfloat16 [32768, 2048], P(('seq', 'sub'))
Inputs may be any that keep to these rules, and one draw needn't show every extreme that they name: `pattern`: each row is an ordering of the 128 positions of a block. `slide_lengths`: the slides lie end to end and fill all 256 blocks. `normed`: entries of order one. `w_query`: entries of order 2048 ** -0.5. `w_key`: entries of order 2048 ** -0.5.
All inputs are finite; a program needn't handle non-finite values.
Results may differ from a plain program's by a relative error of at most 0.012.
Values may be sent and summed in bfloat16 or wider, within the bound.
A program may use at most 128 MiB of HBM per device.

v0:
```python
import math
import jax
import jax.numpy as jnp
from jax import lax
from jax.sharding import PartitionSpec as P

HEAD_SIZE = 128
BLOCK = 128
DILATED_KEPT = 16


def slide_count(block_index, slide_ends):
    return jnp.sum((block_index[:, None] >= slide_ends[None, :]).astype(jnp.int32), axis=1)


def shards(normed, w_query, w_key, w_value, w_out, pattern, slide_lengths):
    head_cols = w_query.shape[1]
    nearby_heads = head_cols // HEAD_SIZE
    piece = lax.all_gather(normed, "sub", axis=0, tiled=True)
    outputs = [
        jnp.dot(piece, weight, preferred_element_type=jnp.float32).astype(jnp.bfloat16)
        for weight in (w_query, w_key, w_value)
    ]
    projected = jnp.concatenate(outputs, axis=1)
    queries = projected[:, :head_cols]
    keys_all = projected[:, head_cols : 2 * head_cols]
    values_all = projected[:, 2 * head_cols :]
    span_len = projected.shape[0]
    span_of_blocks = span_len // BLOCK
    my_span = lax.axis_index("seq")
    slide_ends = jnp.cumsum(slide_lengths)
    kept_positions = pattern[:, :DILATED_KEPT]

    def dilate(source):
        blocked = source.reshape(span_of_blocks, BLOCK, nearby_heads, HEAD_SIZE)
        selected_keys = [
            blocked[:, kept_positions[head_index], head_index, :]
            for head_index in range(nearby_heads)
        ]
        return jnp.stack(selected_keys).reshape(
            nearby_heads, span_of_blocks * DILATED_KEPT, HEAD_SIZE
        )

    far_keys, far_values = (
        lax.all_gather(dilate(keys_all), "seq", axis=1, tiled=True),
        lax.all_gather(dilate(values_all), "seq", axis=1, tiled=True),
    )
    distant_count = far_keys.shape[1]
    distant_block = jnp.arange(distant_count, dtype=jnp.int32) // DILATED_KEPT
    distant_slide = slide_count(distant_block, slide_ends)
    far_span = distant_block // span_of_blocks
    row_block = my_span * span_of_blocks + jnp.arange(span_len, dtype=jnp.int32) // BLOCK
    row_slide = slide_count(row_block, slide_ends)
    near_mask = row_slide[:, None] == row_slide[None, :]
    far_mask = (row_slide[:, None] == distant_slide[None, :]) & (far_span != my_span)[None, :]
    scale = 1.0 / math.sqrt(HEAD_SIZE)
    outputs = []
    for head_index in range(nearby_heads):
        columns = slice(head_index * HEAD_SIZE, (head_index + 1) * HEAD_SIZE)
        query_head = queries[:, columns]
        near = (
            jnp.einsum(
                "qd,kd->qk", query_head, keys_all[:, columns], preferred_element_type=jnp.float32
            )
            * scale
        )
        far = (
            jnp.einsum(
                "qd,kd->qk", query_head, far_keys[head_index], preferred_element_type=jnp.float32
            )
            * scale
        )
        near = jnp.where(near_mask, near, -1e30)
        far = jnp.where(far_mask, far, -1e30)
        peak = jnp.maximum(
            jnp.max(near, axis=1, keepdims=True), jnp.max(far, axis=1, keepdims=True)
        )
        near_exp = jnp.exp(near - peak)
        far_exp = jnp.exp(far - peak)
        total = jnp.sum(near_exp, axis=1, keepdims=True) + jnp.sum(far_exp, axis=1, keepdims=True)
        near_weight = (near_exp / total).astype(jnp.bfloat16)
        far_weight = (far_exp / total).astype(jnp.bfloat16)
        context_head = jnp.dot(
            near_weight, values_all[:, columns], preferred_element_type=jnp.float32
        )
        context_head = context_head + jnp.dot(
            far_weight, far_values[head_index], preferred_element_type=jnp.float32
        )
        outputs.append(context_head.astype(jnp.bfloat16))
    context = jnp.concatenate(outputs, axis=1)
    return lax.psum_scatter(
        jnp.dot(context, w_out, preferred_element_type=jnp.float32),
        "sub",
        scatter_dimension=0,
        tiled=True,
    ).astype(jnp.bfloat16)


def solution(mesh):
    placed = (
        P(("seq", "sub"), None),
        P(None, "sub"),
        P(None, "sub"),
        P(None, "sub"),
        P("sub", None),
        P("sub", None),
        P(),
    )
    return jax.shard_map(
        shards, mesh=mesh, in_specs=placed, out_specs=P(("seq", "sub"), None), check_vma=False
    )
```

profile of v0, /device:TPU:1, one launch (start us, length us, event | category | flops | bytes accessed | tf_op | source)
XLA Modules:
  0.0 747.7 jit_solution(3258712888125607824)
XLA Ops:
  6.5 0.7 all-gather.4.cloned.1.call-update
  7.3 0.8 fusion.52
  8.2 34.3 %all-gather.4.cloned.1.call-done = bf16[512,2048]{1,0:T(8,128)(2,1)} async-done(((bf16[128,2048]{1,0:T(8,128)(2,1)}), bf16[512,2048]{1,0:T(8,128)(2,1)}) %all-gather.4.cloned.1.call-update) | async-done | bytes 2097168 | tf_op jit(solution)/shard_map/all_gather | solution.py:19
  42.5 3.5 convolution_convert_fusion.1
  46.0 0.8 copy-done.8
  46.9 0.7 copy.32
  50.8 3.5 convolution_convert_fusion
  54.3 0.8 copy-done.6
  59.5 3.5 convolution_convert_fusion.2
  63.0 2.4 fusion.72
  65.4 1.3 fusion.70
  66.7 1.3 fusion.68
  68.0 1.2 fusion.66
  69.3 238.2 %all-gather.6.cloned.1.call-done = bf16[4,4096,128]{2,1,0:T(8,128)(2,1)} async-done(((bf16[4,64,128]{2,1,0:T(8,128)(2,1)}), bf16[4,4096,128]{2,1,0:T(8,128)(2,1)}) %all-gather.6.cloned.1.call-update) | async-done | bytes 4194320 | tf_op jit(solution)/shard_map/all_gather | solution.py:45
  307.5 3.8 fusion.73
  311.5 3.0 copy-done.1
  314.5 1.3 fusion
  315.8 294.4 %all-gather.8.cloned.1.call-done = bf16[4,4096,128]{2,1,0:T(8,128)(2,1)} async-done(((bf16[4,64,128]{2,1,0:T(8,128)(2,1)}), bf16[4,4096,128]{2,1,0:T(8,128)(2,1)}) %all-gather.8.cloned.1.call-update) | async-done | bytes 4194320 | tf_op jit(solution)/shard_map/all_gather | solution.py:46
  610.1 5.2 fusion.4
  615.7 2.4 fusion.71
  618.2 1.3 fusion.1
  619.6 1.0 copy-done.11
  620.6 2.1 fusion.5
  623.1 2.4 fusion.69
  625.5 1.3 fusion.2
  627.0 2.1 fusion.6
  629.4 2.6 fusion.67
  632.0 1.3 fusion.3
  633.5 2.1 fusion.7
  635.9 3.2 fusion.16
  639.2 99.9 %reduce-scatter.2.cloned.1.call-done = f32[128,2048]{1,0:T(8,128)} async-done(((f32[512,2048]{1,0:T(8,128)}), f32[128,2048]{1,0:T(8,128)}) %reduce-scatter.2.cloned.1.call-update) | async-done | bytes 1048592 | tf_op jit(solution)/shard_map/reduce_scatter | solution.py:91
  739.1 2.1 convert_element_type.71
  (76 shorter events, 10.0 us)
Async XLA Ops:
  6.5 629.4 %copy-start = (bf16[512,2048]{1,0:T(8,128)(2,1)S(1)}, bf16[512,2048]{1,0:T(8,128)(2,1)}, u32[]{:S(2)}) copy-start(bf16[512,2048]{1,0:T(8,128)(2,1)} %param.11) | copy-start | bytes 6291460
  6.5 36.0 %all-gather.4.cloned.1.call-start = ((), (), s32[]{:S(2)}) async-start(), calls=%async_computation.1 | async-start | bytes 2621440 | tf_op jit(solution)/shard_map/all_gather | solution.py:19
  7.3 300.2 %all-gather.6.cloned.1.call-start = ((), (), s32[]{:S(2)}) async-start(), calls=%async_computation.2 | async-start | bytes 4259840 | tf_op jit(solution)/shard_map/all_gather | solution.py:45
  8.1 50.9 %copy-start.12 = (s32[8]{0:T(128)S(1)}, s32[8]{0:T(128)}, u32[]{:S(2)}) copy-start(s32[8]{0:T(128)} %param.13) | copy-start | bytes 100
  46.0 0.8 copy-start.8
  50.7 559.4 %all-gather.8.cloned.1.call-start = ((), (), s32[]{:S(2)}) async-start(), calls=%async_computation.3 | async-start | bytes 4259840 | tf_op jit(solution)/shard_map/all_gather | solution.py:46
  54.3 0.8 copy-start.6
  55.9 9.5 %copy-start.9 = (bf16[512,512]{1,0:T(8,128)(2,1)S(1)}, bf16[512,512]{1,0:T(8,128)(2,1)}, u32[]{:S(2)}) copy-start(bf16[512,512]{1,0:T(8,128)(2,1)} %copy-done.8) | copy-start | bytes 1572868
  59.0 680.0 %reduce-scatter.2.cloned.1.call-start = ((), (), s32[]{:S(2)}) async-start(), calls=%async_computation.4 | async-start | bytes 5242880 | tf_op jit(solution)/shard_map/reduce_scatter | solution.py:91
  63.0 5.0 copy-start.13
  307.5 3.8 copy-start.4
  311.2 3.2 copy-start.1
  610.1 5.2 copy-start.5
  610.1 5.2 copy-start.7
  610.1 5.6 copy-start.10
  610.1 5.6 copy-start.14
  618.1 1.3 copy-start.3
  618.1 2.5 copy-start.11
  625.5 1.3 copy-start.2
Sparse Core Ops, SparseCore 0:
  9.1 33.3 all-gather.3
  50.9 256.5 all-gather.5
  309.3 300.7 all-gather.7
  639.3 99.7 reduce-scatter.1
where the time goes:
time: 748 us
  waiting for transfers between devices  668 us (89%)
  matrix products  43.8 us (6%)
  between operations  13.5 us (2%)
  local copies, waits for them, and re-layouts  12.2 us (2%)
  other arithmetic  10.5 us (1%)
    all_gather x1, waiting for transfers between devices, shards(): lax.all_gather(dilate(values_all), 'seq', axis=1, tiled=True)  294 us
    all_gather x1, waiting for transfers between devices, shards(): lax.all_gather(dilate(keys_all), 'seq', axis=1, tiled=True)  238 us
    reduce_scatter x1, waiting for transfers between devices, shards(): lax.psum_scatter(jnp.dot(context, w_out, preferred_element_type=jnp.float...  99.9 us
    all_gather x1, waiting for transfers between devices, shards(): piece = lax.all_gather(normed, 'sub', axis=0, tiled=True)  34.3 us
  transfers between devices with their start and end apart: 4, of which 4 were waited for; matrix products, arithmetic and copies ran while one was open for 3% of the time, Pallas kernels for 0%

commit v1 on v0

--- a/solution.py
+++ b/solution.py
@@ -43,7 +43,10 @@
 
     far_keys, far_values = (
         lax.all_gather(dilate(keys_all), "seq", axis=1, tiled=True),
-        lax.all_gather(dilate(values_all), "seq", axis=1, tiled=True),
+        jnp.concatenate(
+            lax.all_to_all(jnp.stack([dilate(values_all)] * lax.axis_size("seq")), "seq", 0, 0),
+            axis=1,
+        ),
     )
     distant_count = far_keys.shape[1]
     distant_block = jnp.arange(distant_count, dtype=jnp.int32) // DILATED_KEPT

time: 748 us -> 479 us (0.64)
  waiting for transfers between devices: 668 us -> 387 us
  starting transfers between devices: 0.13 us -> 10.9 us
    all_gather x1 -> x0, waiting for transfers between devices: 294 us -> none  [shards(): lax.all_gather(dilate(values_all), 'seq', axis=1, tiled=True)]
    all_to_all x0 -> x1, waiting for transfers between devices: none -> 85.2 us  [shards(): lax.all_to_all(jnp.stack([dilate(values_all)] * lax.axis_size('seq')), 's...]
    all_gather x1, waiting for transfers between devices: 238 us -> 176 us  [shards(): lax.all_gather(dilate(keys_all), 'seq', axis=1, tiled=True)]
    all_to_all x0 -> x1, starting transfers between devices: none -> 10.6 us  [shards(): lax.all_to_all(jnp.stack([dilate(values_all)] * lax.axis_size('seq')), 's...]
    reduce_scatter x1, waiting for transfers between devices: 99.9 us -> 90.6 us  [shards(): lax.psum_scatter(jnp.dot(context, w_out, preferred_element_type=jnp.float...]
  transfers between devices with their start and end apart: 4 -> 4, of which waited for: 4 -> 4; matrix products, arithmetic and copies ran while one was open for 3% -> 5% of each run, Pallas kernels for 0% -> 0%
where the time goes in v1:
time: 479 us
  waiting for transfers between devices  387 us (81%)
  matrix products  41.8 us (9%)
  local copies, waits for them, and re-layouts  16 us (3%)
  between operations  13.5 us (3%)
  starting transfers between devices  10.9 us (2%)
  other arithmetic  9.89 us (2%)
    all_gather x1, waiting for transfers between devices, shards(): lax.all_gather(dilate(keys_all), 'seq', axis=1, tiled=True)  176 us
    reduce_scatter x1, waiting for transfers between devices, shards(): lax.psum_scatter(jnp.dot(context, w_out, preferred_element_type=jnp.float...  90.6 us
    all_to_all x1, waiting for transfers between devices, shards(): lax.all_to_all(jnp.stack([dilate(values_all)] * lax.axis_size('seq')), 's...  85.2 us
    all_gather x1, waiting for transfers between devices, shards(): piece = lax.all_gather(normed, 'sub', axis=0, tiled=True)  34.4 us
    dot_general x4, matrix products, shards(): jnp.einsum('qd,kd->qk', query_head, far_keys[head_index], preferred_eleme...  10.9 us
    all_to_all x1, starting transfers between devices, shards(): lax.all_to_all(jnp.stack([dilate(values_all)] * lax.axis_size('seq')), 's...  10.6 us
    dot_general x3, matrix products, shards(): jnp.dot(piece, weight, preferred_element_type=jnp.float32)  10.4 us
    dot_general x4, matrix products, shards(): jnp.dot(far_weight, far_values[head_index], preferred_element_type=jnp.fl...  9.63 us
  transfers between devices with their start and end apart: 4, of which 4 were waited for; matrix products, arithmetic and copies ran while one was open for 5% of the time, Pallas kernels for 0%

profile of v1, /device:TPU:1, one launch (start us, length us, event | category | flops | bytes accessed | tf_op | source)
XLA Modules:
  0.0 478.8 jit_solution(9152277677348411887)
XLA Ops:
  6.5 0.7 all-gather.3.cloned.1.call-update
  7.3 0.8 fusion.52
  8.1 34.4 %all-gather.3.cloned.1.call-done = bf16[512,2048]{1,0:T(8,128)(2,1)} async-done(((bf16[128,2048]{1,0:T(8,128)(2,1)}), bf16[512,2048]{1,0:T(8,128)(2,1)}) %all-gather.3.cloned.1.call-update) | async-done | bytes 2097168 | tf_op jit(solution)/shard_map/all_gather | solution.py:19
  42.5 3.5 convolution_convert_fusion
  46.0 0.8 copy-done.8
  50.1 3.0 stack.43
  53.1 10.6 %all-to-all-start = ((bf16[64,4,64,128]{3,2,1,0:T(8,128)(2,1)}), bf16[64,4,64,128]{3,2,1,0:T(8,128)(2,1)}, u32[]{:S(2)}, u32[]{:S(2)}) async-start(bf16[64,4,64,128]{3,2,1,0:T(8,128)(2,1)} %stack.43), calls=%async_computation | async-start | bytes 8388608 | tf_op jit(solution)/shard_map/all_to_all | solution.py:47
  63.8 3.5 convolution_convert_fusion.1
  67.3 0.8 copy-done.10
  72.7 3.5 convolution_convert_fusion.2
  76.2 2.4 fusion.67
  78.6 1.3 fusion.69
  79.8 1.4 fusion.71
  81.2 1.2 fusion.73
  82.4 85.2 %all-to-all-done = bf16[64,4,64,128]{3,2,1,0:T(8,128)(2,1)} async-done(((bf16[64,4,64,128]{3,2,1,0:T(8,128)(2,1)}), bf16[64,4,64,128]{3,2,1,0:T(8,128)(2,1)}, u32[]{:S(2)}, u32[]{:S(2)}) %all-to-all-start) | async-done | bytes 4194336 | tf_op jit(solution)/shard_map/all_to_all | solution.py:47
  167.6 4.8 fusion.66
  172.4 175.7 %all-gather.5.cloned.1.call-done = bf16[4,4096,128]{2,1,0:T(8,128)(2,1)} async-done(((bf16[4,64,128]{2,1,0:T(8,128)(2,1)}), bf16[4,4096,128]{2,1,0:T(8,128)(2,1)}) %all-gather.5.cloned.1.call-update) | async-done | bytes 4194320 | tf_op jit(solution)/shard_map/all_gather | solution.py:45
  348.1 3.8 fusion.68
  352.1 1.3 fusion.3
  353.4 2.5 fusion.7
  356.3 2.4 fusion.70
  358.9 1.3 fusion.2
  360.2 2.3 fusion.6
  362.9 2.4 fusion.72
  365.5 1.3 fusion.1
  366.8 2.5 fusion.5
  369.7 2.4 fusion.74
  372.3 1.3 fusion
  373.6 2.3 fusion.4
  376.3 3.2 fusion.16
  379.5 90.6 %reduce-scatter.2.cloned.1.call-done = f32[128,2048]{1,0:T(8,128)} async-done(((f32[512,2048]{1,0:T(8,128)}), f32[128,2048]{1,0:T(8,128)}) %reduce-scatter.2.cloned.1.call-update) | async-done | bytes 1048592 | tf_op jit(solution)/shard_map/reduce_scatter | solution.py:94
  470.1 2.1 convert_element_type.71
  (79 shorter events, 10.2 us)
Async XLA Ops:
  6.5 369.7 %copy-start = (bf16[512,2048]{1,0:T(8,128)(2,1)S(1)}, bf16[512,2048]{1,0:T(8,128)(2,1)}, u32[]{:S(2)}) copy-start(bf16[512,2048]{1,0:T(8,128)(2,1)} %param.11) | copy-start | bytes 6291460
  6.5 36.0 %all-gather.3.cloned.1.call-start = ((), (), s32[]{:S(2)}) async-start(), calls=%async_computation.2 | async-start | bytes 2621440 | tf_op jit(solution)/shard_map/all_gather | solution.py:19
  46.0 0.8 copy-start.8
  53.1 19.1 %copy-start.13 = (s32[8]{0:T(128)S(1)}, s32[8]{0:T(128)}, u32[]{:S(2)}) copy-start(s32[8]{0:T(128)} %param.13) | copy-start | bytes 100
  53.1 114.5 %all-to-all-start = ((bf16[64,4,64,128]{3,2,1,0:T(8,128)(2,1)}), bf16[64,4,64,128]{3,2,1,0:T(8,128)(2,1)}, u32[]{:S(2)}, u32[]{:S(2)}) async-start(bf16[64,4,64,128]{3,2,1,0:T(8,128)(2,1)} %stack.43), calls=%async_computation | async-start | bytes 8388608 | tf_op jit(solution)/shard_map/all_to_all | solution.py:47
  63.7 284.4 %all-gather.5.cloned.1.call-start = ((), (), s32[]{:S(2)}) async-start(), calls=%async_computation.3 | async-start | bytes 4259840 | tf_op jit(solution)/shard_map/all_gather | solution.py:45
  67.3 0.8 copy-start.10
  68.9 9.7 %copy-start.11 = (bf16[512,512]{1,0:T(8,128)(2,1)S(1)}, bf16[512,512]{1,0:T(8,128)(2,1)}, u32[]{:S(2)}) copy-start(bf16[512,512]{1,0:T(8,128)(2,1)} %copy-done.10) | copy-start | bytes 1572868
  72.0 398.1 %reduce-scatter.2.cloned.1.call-start = ((), (), s32[]{:S(2)}) async-start(), calls=%async_computation.4 | async-start | bytes 5242880 | tf_op jit(solution)/shard_map/reduce_scatter | solution.py:94
  76.2 5.0 %copy-start.14 = (bf16[512,512]{1,0:T(8,128)(2,1)}, bf16[512,512]{1,0:T(8,128)(2,1)S(1)}, u32[]{:S(2)}) copy-start(bf16[512,512]{1,0:T(8,128)(2,1)S(1)} %convolution_convert_fusion.2) | copy-start | bytes 1572868
  348.1 3.8 copy-start.3
  351.9 1.5 copy-start.7
  353.4 2.6 copy-start.9
  353.4 2.9 copy-start.12
  353.4 2.9 copy-start.15
  356.3 2.4 copy-start.2
  358.7 1.5 copy-start.6
  362.9 2.4 copy-start.1
  365.3 1.5 copy-start.5
  372.1 1.5 copy-start.4
Sparse Core Ops, SparseCore 0:
  9.1 33.3 all-gather.2
  72.2 275.9 all-gather.4
  379.6 90.4 reduce-scatter.1
